TPU v7x, 32 devices: a whole 2x2x4 slice. The times are simulated.
32 devices in a mesh: row: 8 (over z, core), col: 4 (over y, x).
Axes of the slice: x: 2, y: 2, z: 4, core: 2. Of those that a mesh axis runs over, the one named last changes fastest.
Arguments:
- tokens: bfloat16 [16384, 1024], P('row', 'col'), may hold values from -6 to 6
- memory: bfloat16 [4096, 1024], P('row', 'col'), may hold values from -6 to 6
- old_memory: bfloat16 [12288, 1024], P('row', 'col'), may hold values from -6 to 6
- doc_ids: int32 [8, 4096], P('row'), may hold values from 0 to 5, as said below
- norm_gains: bfloat16 [2, 1024], P(None, 'row'), may hold values from 0.5 to 1.5
- comp_weight: bfloat16 [3072, 1024], P('row', 'col'), may hold values from -0.109375 to 0.109375
- query_weight: bfloat16 [1024, 1024], P('row', 'col'), may hold values from -0.1875 to 0.1875
- key_weight: bfloat16 [1024, 1024], P('row', 'col'), may hold values from -0.1875 to 0.1875
- value_weight: bfloat16 [1024, 1024], P('row', 'col'), may hold values from -0.1875 to 0.1875
- proj_weight: bfloat16 [1024, 1024], P('col', 'row'), may hold values from -1.5 to 1.5
- up_weight: bfloat16 [1024, 4096], P('row', 'col'), may hold values from -0.1875 to 0.1875
- down_weight: bfloat16 [4096, 1024], P('col', 'row'), may hold values from -0.09375 to 0.09375
- cotangent: bfloat16 [16384, 1024], P('row', 'col'), may hold values from -6 to 6
Outputs:
- layer_out: bfloat16 [16384, 1024], P('row', 'col')
- grad_x: float32 [16384, 1024], P('row', 'col')
- grad_gains: float32 [2, 1024], P(None, 'row')
- grad_comp: float32 [3072, 1024], P('row', 'col')
- grad_query: float32 [1024, 1024], P('row', 'col')
- grad_key: float32 [1024, 1024], P('row', 'col')
- grad_value: float32 [1024, 1024], P('row', 'col')
- grad_proj: float32 [1024, 1024], P('col', 'row')
- grad_up: float32 [1024, 4096], P('row', 'col')
- grad_down: float32 [4096, 1024], P('col', 'row')
Inputs may be any that keep to these rules, and one draw needn't show every extreme that they name: In each row of doc_ids the numbers never fall and every number occurs; every document covers 200 entries or more.
All inputs are finite; a program needn't handle non-finite values.
Results may differ from a plain program's by a relative error of at most 0.015.
Values may be sent and summed in bfloat16 or wider, within the bound.
A program may use at most 192 MiB of HBM per device.

v0:
```python
import jax
import jax.numpy as jnp
from jax import lax
from jax.sharding import PartitionSpec as P

RATE = 3
HD = 128


def normalize(rows, gain):
    centre = rows - jnp.mean(rows, axis=-1, keepdims=True)
    spread = jnp.mean(centre * centre, axis=-1, keepdims=True)
    return centre * lax.rsqrt(spread + 1e-05) * gain


def contract_rows(left, right):
    return lax.dot_general(
        left, right, (((0,), (0,)), ((), ())), preferred_element_type=jnp.float32
    )


def contract_cols(left, right):
    return lax.dot_general(
        left, right, (((1,), (1,)), ((), ())), preferred_element_type=jnp.float32
    )


def on_device(
    tokens,
    memory,
    old_memory,
    doc_ids,
    norm_gains,
    comp_weight,
    query_weight,
    key_weight,
    value_weight,
    proj_weight,
    up_weight,
    down_weight,
    cotangent,
):
    full_tokens, full_memory, full_old, full_grad = (
        lax.all_gather(tokens, "col", axis=1, tiled=True),
        lax.all_gather(memory, "col", axis=1, tiled=True),
        lax.all_gather(old_memory, "col", axis=1, tiled=True),
        lax.all_gather(cotangent, "col", axis=1, tiled=True),
    )
    comp_full, query_full, key_full, value_full, up_full = (
        lax.all_gather(comp_weight, "row", axis=0, tiled=True),
        lax.all_gather(query_weight, "row", axis=0, tiled=True),
        lax.all_gather(key_weight, "row", axis=0, tiled=True),
        lax.all_gather(value_weight, "row", axis=0, tiled=True),
        lax.all_gather(up_weight, "row", axis=0, tiled=True),
    )
    proj_full, down_full, gain_full = (
        lax.all_gather(proj_weight, "row", axis=1, tiled=True),
        lax.all_gather(down_weight, "row", axis=1, tiled=True),
        lax.all_gather(norm_gains, "row", axis=1, tiled=True),
    )
    width = full_tokens.shape[1]
    slab = tokens.shape[1]
    column = lax.axis_index("col")
    seq_len = tokens.shape[0]
    mem_len = memory.shape[0]
    comp_len = old_memory.shape[0] // RATE
    start_tok = comp_len + mem_len
    all_keys = start_tok + seq_len
    gain_one = gain_full[0].astype(jnp.float32)
    gain_two = gain_full[1].astype(jnp.float32)
    old_rows = full_old.reshape(comp_len, RATE * width)
    compressed = jnp.dot(old_rows, comp_full, preferred_element_type=jnp.float32).astype(
        jnp.bfloat16
    )
    compressed_all = lax.all_gather(compressed, "col", axis=1, tiled=True)
    stacked = jnp.concatenate([compressed_all, full_memory, full_tokens], axis=0).astype(
        jnp.float32
    )
    normed = normalize(stacked, gain_one).astype(jnp.bfloat16)
    queries = jnp.dot(normed[start_tok:], query_full, preferred_element_type=jnp.float32).astype(
        jnp.bfloat16
    )
    keys = jnp.dot(normed, key_full, preferred_element_type=jnp.float32).astype(jnp.bfloat16)
    values = jnp.dot(normed, value_full, preferred_element_type=jnp.float32).astype(jnp.bfloat16)
    local_heads = queries.shape[1] // HD
    key_heads = keys.reshape(all_keys, local_heads, HD)
    value_heads = values.reshape(all_keys, local_heads, HD)
    doc_row = doc_ids[0]
    key_doc = jnp.concatenate(
        [doc_row[RATE - 1 : RATE * comp_len : RATE], doc_row[RATE * comp_len :]]
    )
    key_place = jnp.arange(all_keys, dtype=jnp.int32) - start_tok
    query_doc = doc_row[RATE * comp_len + mem_len :]
    query_place = jnp.arange(seq_len, dtype=jnp.int32)
    block = min(512, seq_len)
    steps_count = seq_len // block
    scale = HD ** (-0.5)
    query_blocks = queries.reshape(steps_count, block, local_heads, HD)
    doc_blocks = query_doc.reshape(steps_count, block)
    place_blocks = query_place.reshape(steps_count, block)

    def masked_scores(query_block, doc_block, place_block):
        allowed = (doc_block[:, None] == key_doc[None, :]) & (
            key_place[None, :] <= place_block[:, None]
        )
        scores = (
            jnp.einsum("qhd,khd->hqk", query_block, key_heads, preferred_element_type=jnp.float32)
            * scale
        )
        return jnp.where(allowed[None], scores, -1e30)

    def forward_block(items):
        query_block, doc_block, place_block = items
        scores = masked_scores(query_block, doc_block, place_block)
        top = jnp.max(scores, axis=-1, keepdims=True)
        raw = jnp.exp(scores - top)
        total = jnp.sum(raw, axis=-1, keepdims=True)
        rounded = (raw / total).astype(jnp.bfloat16)
        mixed_block = jnp.einsum(
            "hqk,khd->qhd", rounded, value_heads, preferred_element_type=jnp.float32
        )
        return (mixed_block, top, total)

    mixed_blocks, tops, totals = lax.map(forward_block, (query_blocks, doc_blocks, place_blocks))
    mixed = mixed_blocks.reshape(seq_len, local_heads * HD).astype(jnp.bfloat16)
    branch = lax.psum(jnp.dot(mixed, proj_full, preferred_element_type=jnp.float32), "col")
    resid = full_tokens.astype(jnp.float32) + branch
    hidden_in = normalize(resid, gain_two).astype(jnp.bfloat16)
    upper = jnp.dot(hidden_in, up_full, preferred_element_type=jnp.float32)
    active = jax.nn.gelu(upper).astype(jnp.bfloat16)
    down_terms = jnp.dot(active, down_full, preferred_element_type=jnp.float32)
    final = resid + lax.psum(down_terms.astype(jnp.bfloat16), "col").astype(jnp.float32)
    layer_out = lax.dynamic_slice_in_dim(final, column * slab, slab, 1).astype(jnp.bfloat16)
    grad_down = contract_rows(active, full_grad)
    grad_active = contract_cols(full_grad, down_full)
    _, gelu_pull = jax.vjp(jax.nn.gelu, upper)
    grad_upper = gelu_pull(grad_active)[0].astype(jnp.bfloat16)
    grad_up = contract_rows(hidden_in, grad_upper)
    grad_hidden = lax.psum(contract_cols(grad_upper, up_full), "col")
    _, second_pull = jax.vjp(normalize, resid, gain_two)
    grad_resid_norm, grad_gain_two = second_pull(grad_hidden)
    grad_resid = full_grad.astype(jnp.float32) + grad_resid_norm
    grad_branch = grad_resid.astype(jnp.bfloat16)
    grad_proj = contract_rows(mixed, grad_branch)
    grad_mixed = contract_cols(grad_branch, proj_full).astype(jnp.bfloat16)
    grad_blocks = grad_mixed.reshape(steps_count, block, local_heads, HD)

    def backward_block(carry, items):
        grad_keys, grad_values = carry
        query_block, doc_block, place_block, top, total, grad_out = items
        scores = masked_scores(query_block, doc_block, place_block)
        probs = jnp.exp(scores - top) / total
        rounded = probs.astype(jnp.bfloat16)
        grad_probs = jnp.einsum(
            "qhd,khd->hqk", grad_out, value_heads, preferred_element_type=jnp.float32
        )
        grad_scores = (
            probs * (grad_probs - jnp.sum(probs * grad_probs, axis=-1, keepdims=True))
        ).astype(jnp.bfloat16)
        grad_query_block = (
            jnp.einsum("hqk,khd->qhd", grad_scores, key_heads, preferred_element_type=jnp.float32)
            * scale
        )
        grad_keys = (
            grad_keys
            + jnp.einsum(
                "hqk,qhd->khd", grad_scores, query_block, preferred_element_type=jnp.float32
            )
            * scale
        )
        grad_values = grad_values + jnp.einsum(
            "hqk,qhd->khd", rounded, grad_out, preferred_element_type=jnp.float32
        )
        return ((grad_keys, grad_values), grad_query_block)

    empty = jnp.zeros((all_keys, local_heads, HD), jnp.float32)
    (grad_key_heads, grad_value_heads), grad_query_blocks = lax.scan(
        backward_block,
        (empty, empty),
        (query_blocks, doc_blocks, place_blocks, tops, totals, grad_blocks),
    )
    grad_queries = grad_query_blocks.reshape(seq_len, local_heads * HD).astype(jnp.bfloat16)
    grad_keys_low = grad_key_heads.reshape(all_keys, local_heads * HD).astype(jnp.bfloat16)
    grad_values_low = grad_value_heads.reshape(all_keys, local_heads * HD).astype(jnp.bfloat16)
    grad_query = contract_rows(normed[start_tok:], grad_queries)
    grad_key = contract_rows(normed, grad_keys_low)
    grad_value = contract_rows(normed, grad_values_low)
    back_keys = contract_cols(grad_keys_low, key_full) + contract_cols(grad_values_low, value_full)
    back_queries = contract_cols(grad_queries, query_full)
    partial_rows = jnp.concatenate(
        [back_keys[:start_tok], back_keys[start_tok:] + back_queries], axis=0
    )
    grad_normed = lax.psum(partial_rows, "col")
    _, first_pull = jax.vjp(normalize, stacked, gain_one)
    grad_stacked, grad_gain_one = first_pull(grad_normed)
    grad_comp_slab = lax.dynamic_slice_in_dim(grad_stacked[:comp_len], column * slab, slab, 1)
    grad_tok_slab = lax.dynamic_slice_in_dim(grad_stacked[start_tok:], column * slab, slab, 1)
    grad_x = lax.dynamic_slice_in_dim(grad_resid, column * slab, slab, 1) + grad_tok_slab
    grad_comp_low = grad_comp_slab.astype(jnp.bfloat16)
    grad_comp = contract_rows(old_rows, grad_comp_low)
    grad_gains = jnp.stack([grad_gain_one, grad_gain_two], axis=0)
    comp_part, query_part, key_part, value_part, up_part = (
        lax.psum_scatter(grad_comp, "row", scatter_dimension=0, tiled=True),
        lax.psum_scatter(grad_query, "row", scatter_dimension=0, tiled=True),
        lax.psum_scatter(grad_key, "row", scatter_dimension=0, tiled=True),
        lax.psum_scatter(grad_value, "row", scatter_dimension=0, tiled=True),
        lax.psum_scatter(grad_up, "row", scatter_dimension=0, tiled=True),
    )
    proj_part, down_part, gains_part = (
        lax.psum_scatter(grad_proj, "row", scatter_dimension=1, tiled=True),
        lax.psum_scatter(grad_down, "row", scatter_dimension=1, tiled=True),
        lax.psum_scatter(grad_gains, "row", scatter_dimension=1, tiled=True),
    )
    return (
        layer_out,
        grad_x,
        gains_part,
        comp_part,
        query_part,
        key_part,
        value_part,
        proj_part,
        up_part,
        down_part,
    )


def solution(mesh):
    in_specs = (
        P("row", "col"),
        P("row", "col"),
        P("row", "col"),
        P("row", None),
        P(None, "row"),
        P("row", "col"),
        P("row", "col"),
        P("row", "col"),
        P("row", "col"),
        P("col", "row"),
        P("row", "col"),
        P("col", "row"),
        P("row", "col"),
    )
    out_specs = (
        P("row", "col"),
        P("row", "col"),
        P(None, "row"),
        P("row", "col"),
        P("row", "col"),
        P("row", "col"),
        P("row", "col"),
        P("col", "row"),
        P("row", "col"),
        P("col", "row"),
    )
    return jax.shard_map(
        on_device, mesh=mesh, in_specs=in_specs, out_specs=out_specs, check_vma=False
    )
```

profile of v0, /device:TPU:0, one launch (start us, length us, event | category | flops | bytes accessed | tf_op | source)
XLA Modules:
  0.0 1541.5 jit_solution(4942058512463735601)
XLA Ops:
  10.1 46.2 %all-gather.11.cloned.1.call-done = bf16[1536,1024]{1,0:T(8,128)(2,1)} async-done(((bf16[1536,256]{1,0:T(8,128)(2,1)}), bf16[1536,1024]{1,0:T(8,128)(2,1)}) %all-gather.11.cloned.1.call-update) | async-done | bytes 3145744 | tf_op jit(solution)/shard_map/all_gather | solution.py:46
  60.6 22.7 %all-gather.13.cloned.1.call-done = bf16[3072,256]{1,0:T(8,128)(2,1)} async-done(((bf16[384,256]{1,0:T(8,128)(2,1)}), bf16[3072,256]{1,0:T(8,128)(2,1)}) %all-gather.13.cloned.1.call-update) | async-done | bytes 1572880 | tf_op jit(solution)/shard_map/all_gather | solution.py:50
  88.0 9.9 all_gather.44
  98.6 15.8 %all_gather.45 = bf16[1024,256]{1,0:T(8,128)(2,1)} all-gather(bf16[128,256]{1,0:T(8,128)(2,1)S(1)} %copy-done.47), channel_id=1, replica_groups=mesh['row'=8,'col'=4] {'row'}, dimensions={0}, use_global_device_ids=true | all-gather | bytes 589824 | tf_op jit(solution)/shard_map/all_gather | solution.py:51
  114.4 15.8 %all_gather.46 = bf16[1024,256]{1,0:T(8,128)(2,1)} all-gather(bf16[128,256]{1,0:T(8,128)(2,1)S(1)} %copy-done.48), channel_id=1, replica_groups=mesh['row'=8,'col'=4] {'row'}, dimensions={0}, use_global_device_ids=true | all-gather | bytes 589824 | tf_op jit(solution)/shard_map/all_gather | solution.py:52
  130.2 15.8 %all_gather.47 = bf16[1024,256]{1,0:T(8,128)(2,1)} all-gather(bf16[128,256]{1,0:T(8,128)(2,1)S(1)} %copy-done.49), channel_id=1, replica_groups=mesh['row'=8,'col'=4] {'row'}, dimensions={0}, use_global_device_ids=true | all-gather | bytes 589824 | tf_op jit(solution)/shard_map/all_gather | solution.py:53
  146.1 15.2 all_gather.48
  164.8 28.6 %all-gather.15.cloned.1.call-done = bf16[512,1024]{1,0:T(8,128)(2,1)} async-done(((bf16[512,256]{1,0:T(8,128)(2,1)}), bf16[512,1024]{1,0:T(8,128)(2,1)}) %all-gather.15.cloned.1.call-update) | async-done | bytes 1048592 | tf_op jit(solution)/shard_map/all_gather | solution.py:75
  232.0 61.1 %while.30 = (s32[]{:T(128)}, bf16[4,512,2,128]{3,1,2,0:T(8,128)(2,1)}, f32[4,2,512,1]{2,1,3,0:T(2,128)S(1)}, f32[4,2,512,1]{2,1,3,0:T(2,128)S(1)}, s32[4,512]{1,...) while((s32[]{:T(128)}, ...), condition=%wide.region_5.6_spmd.clone, body=%wide.region_2.5_spmd.clone.sunk | while | flops 1653081088 | bytes 56447168 | solution.py:124
  303.6 10.7 fusion.78
  314.3 160.6 %all-reduce.5.cloned.1.call-done = f32[2048,1024]{1,0:T(8,128)} async-done(((f32[2048,1024]{1,0:T(8,128)}), f32[2048,1024]{1,0:T(8,128)}) %all-reduce.5.cloned.1.call-update) | async-done | bytes 8388624 | tf_op jit(solution)/shard_map/psum | solution.py:126
  486.3 20.1 %all-gather.19.cloned.1.call-done = bf16[1024,1024]{1,0:T(8,128)(2,1)} async-done(((bf16[128,1024]{1,0:T(8,128)(2,1)}), bf16[1024,1024]{1,0:T(8,128)(2,1)}) %all-gather.19.cloned.1.call-update) | async-done | bytes 2097168 | tf_op jit(solution)/shard_map/all_gather | solution.py:54
  506.4 16.1 %fusion.50 = (bf16[2048,1024]{1,0:T(8,128)(2,1)S(1)}, f32[2048,1024]{1,0:T(8,128)}) fusion(f32[2048,1024]{1,0:T(8,128)} %fusion.78, bf16[2048,1024]{1,0:T(8,128)(2,1)} %multiply_convert_fusion.2, bf16[1024,1024]{1,0:T(8,128)(2,1)} %all-gather.19.cloned.1.call-done), kind=kOutput, calls=%fused_computation.73 | convolution fusion | flops 4336910336 | bytes 27262976 | tf_op jit(solution)/shard_map/dot_general | solution.py:129
  531.6 171.5 %all-reduce.9.cloned.1.call-done = f32[2048,1024]{1,0:T(8,128)} async-done(((f32[2048,1024]{1,0:T(8,128)}), f32[2048,1024]{1,0:T(8,128)}) %all-reduce.9.cloned.1.call-update) | async-done | bytes 8388624 | tf_op jit(solution)/shard_map/psum | solution.py:139
  726.2 122.1 %while.31 = (s32[]{:T(128)}, f32[3072,2,128]{0,2,1:T(8,128)S(1)}, f32[3072,2,128]{0,2,1:T(8,128)}, bf16[4,512,2,128]{3,1,2,0:T(8,128)(2,1)}, bf16[4,512,2,128]{3...) while((s32[]{:T(128)}, f32[3072,2,128]{0,2,1:T(8,128)S(1)}, ...), condition=%wide.region_15.16_spmd.clone, body=%wide.region_13.15_spmd.clone.sunk | while | flops 4066772992 | bytes 161038704 | solution.py:177
  863.4 11.9 pad_maximum_fusion
  875.6 11.8 convolution_convert_fusion.2
  887.5 227.9 %all-reduce.11.cloned.1.call-done = f32[3072,1024]{1,0:T(8,128)} async-done(((f32[3072,1024]{1,0:T(8,128)}), f32[3072,1024]{1,0:T(8,128)}) %all-reduce.11.cloned.1.call-update) | async-done | bytes 12582928 | tf_op jit(solution)/shard_map/psum | solution.py:193
  1115.5 9.9 fusion.43
  1126.9 11.9 fusion.41
  1139.9 11.5 broadcast_add_fusion
  1161.4 10.2 fusion.83
  1171.6 12.3 fusion.74
  1206.9 15.3 all-reduce.7.cloned.1.call-done
  1232.0 23.9 %reduce-scatter.25.cloned.1.call-done = f32[128,2]{1,0:T(8,128)} async-done(((f32[1024,2]{1,0:T(8,128)}), f32[128,2]{1,0:T(8,128)}) %reduce-scatter.25.cloned.1.call-update) | async-done | bytes 1040
  1257.4 39.2 %reduce-scatter.11.cloned.1.call-done = f32[384,256]{0,1:T(8,128)} async-done(((f32[3072,256]{0,1:T(8,128)}), f32[384,256]{0,1:T(8,128)}) %reduce-scatter.11.cloned.1.call-update) | async-done | bytes 393232 | tf_op jit(solution)/shard_map/reduce_scatter | solution.py:203
  1298.6 50.2 %reduce-scatter.21.cloned.1.call-done = f32[128,1024]{1,0:T(8,128)} async-done(((f32[1024,1024]{1,0:T(8,128)}), f32[128,1024]{1,0:T(8,128)}) %reduce-scatter.21.cloned.1.call-update) | async-done | bytes 524304 | tf_op jit(solution)/shard_map/reduce_scatter | solution.py:207
  1348.7 51.1 %reduce-scatter.23.cloned.1.call-done = f32[1024,128]{1,0:T(8,128)} async-done(((f32[1024,1024]{1,0:T(8,128)}), f32[1024,128]{1,0:T(8,128)}) %reduce-scatter.23.cloned.1.call-update) | async-done | bytes 524304 | tf_op jit(solution)/shard_map/reduce_scatter | solution.py:211
  1399.8 33.8 %reduce-scatter.19.cloned.1.call-done = f32[256,128]{1,0:T(8,128)} async-done(((f32[256,1024]{1,0:T(8,128)}), f32[256,128]{1,0:T(8,128)}) %reduce-scatter.19.cloned.1.call-update) | async-done | bytes 131088 | tf_op jit(solution)/shard_map/reduce_scatter | solution.py:210
  1433.7 33.6 %reduce-scatter.13.cloned.1.call-done = f32[128,256]{1,0:T(8,128)} async-done(((f32[1024,256]{1,0:T(8,128)}), f32[128,256]{1,0:T(8,128)}) %reduce-scatter.13.cloned.1.call-update) | async-done | bytes 131088 | tf_op jit(solution)/shard_map/reduce_scatter | solution.py:204
  1467.2 33.8 %reduce-scatter.15.cloned.1.call-done = f32[128,256]{1,0:T(8,128)} async-done(((f32[1024,256]{1,0:T(8,128)}), f32[128,256]{1,0:T(8,128)}) %reduce-scatter.15.cloned.1.call-update) | async-done | bytes 131088 | tf_op jit(solution)/shard_map/reduce_scatter | solution.py:205
  1501.0 33.5 %reduce-scatter.17.cloned.1.call-done = f32[128,256]{1,0:T(8,128)} async-done(((f32[1024,256]{1,0:T(8,128)}), f32[128,256]{1,0:T(8,128)}) %reduce-scatter.17.cloned.1.call-update) | async-done | bytes 131088 | tf_op jit(solution)/shard_map/reduce_scatter | solution.py:206
  (347 shorter events, 353.9 us)
Async XLA Ops:
  7.2 91.4 %copy-start.47 = (bf16[128,256]{1,0:T(8,128)(2,1)S(1)}, bf16[128,256]{1,0:T(8,128)(2,1)}, u32[]{:S(2)}) copy-start(bf16[128,256]{1,0:T(8,128)(2,1)} %param.23) | copy-start | bytes 196612
  7.2 107.2 %copy-start.48 = (bf16[128,256]{1,0:T(8,128)(2,1)S(1)}, bf16[128,256]{1,0:T(8,128)(2,1)}, u32[]{:S(2)}) copy-start(bf16[128,256]{1,0:T(8,128)(2,1)} %param.24) | copy-start | bytes 196612
  7.2 49.1 %all-gather.11.cloned.1.call-start = ((), (), s32[]{:S(2)}) async-start(), calls=%async_computation.9 | async-start | bytes 3932160 | tf_op jit(solution)/shard_map/all_gather | solution.py:46
  8.0 122.3 %copy-start.49 = (bf16[128,256]{1,0:T(8,128)(2,1)S(1)}, bf16[128,256]{1,0:T(8,128)(2,1)}, u32[]{:S(2)}) copy-start(bf16[128,256]{1,0:T(8,128)(2,1)} %param.25) | copy-start | bytes 196612
  8.0 75.3 %all-gather.13.cloned.1.call-start = ((), (), s32[]{:S(2)}) async-start(), calls=%async_computation.10 | async-start | bytes 1769472 | tf_op jit(solution)/shard_map/all_gather | solution.py:50
  8.7 152.6 %all-gather.17.cloned.1.call-start = ((), (), s32[]{:S(2)}) async-start(), calls=%async_computation.12 | async-start | bytes 1310720 | tf_op jit(solution)/shard_map/all_gather | solution.py:45
  9.4 136.6 %copy-start.50 = (bf16[256,128]{1,0:T(8,128)(2,1)S(1)}, bf16[256,128]{1,0:T(8,128)(2,1)}, u32[]{:S(2)}) copy-start(bf16[256,128]{1,0:T(8,128)(2,1)} %param.26) | copy-start | bytes 196612
  9.5 155.3 %all-gather.9.cloned.1.call-start = ((), (), s32[]{:S(2)}) async-start(), calls=%async_computation.8 | async-start | bytes 5242880 | tf_op jit(solution)/shard_map/all_gather | solution.py:44
  10.0 183.4 %all-gather.15.cloned.1.call-start = ((), (), s32[]{:S(2)}) async-start(), calls=%async_computation.11 | async-start | bytes 1310720 | tf_op jit(solution)/shard_map/all_gather | solution.py:75
  60.5 100.8 %copy-start.19 = (bf16[512,3072]{1,0:T(8,128)(2,1)}, bf16[512,3072]{1,0:T(8,128)(2,1)S(1)}, u32[]{:S(2)}) copy-start(bf16[512,3072]{1,0:T(8,128)(2,1)S(1)} %reshape.251) | copy-start | bytes 9437188
  86.4 217.2 %all-gather.21.cloned.1.call-start = ((), (), s32[]{:S(2)}) async-start(), calls=%async_computation.15 | async-start | bytes 2359296 | tf_op jit(solution)/shard_map/all_gather | solution.py:58
  86.9 216.6 %all-gather.23.cloned.1.call-start = ((), (), s32[]{:S(2)}) async-start(), calls=%async_computation.17 | async-start | bytes 5242880 | tf_op jit(solution)/shard_map/all_gather | solution.py:47
  87.7 387.2 %all-reduce.5.cloned.1.call-start = ((), (), s32[]{:S(2)}) async-start(), calls=%async_computation.13 | async-start | bytes 16777216 | tf_op jit(solution)/shard_map/psum | solution.py:126
  98.5 111.4 %copy-start.45 = (f32[1,1024]{1,0:T(1,128)}, f32[1,1024]{1,0:T(1,128)S(1)}, u32[]{:S(2)}) copy-start(f32[1,1024]{1,0:T(1,128)S(1)} %get-tuple-element.379) | copy-start | bytes 12292
  302.8 203.6 %all-gather.19.cloned.1.call-start = ((), (), s32[]{:S(2)}) async-start(), calls=%async_computation.14 | async-start | bytes 2359296 | tf_op jit(solution)/shard_map/all_gather | solution.py:54
  303.5 399.6 %all-reduce.9.cloned.1.call-start = ((), (), s32[]{:S(2)}) async-start(), calls=%async_computation.18 | async-start | bytes 16777216 | tf_op jit(solution)/shard_map/psum | solution.py:139
  531.5 583.9 %all-reduce.11.cloned.1.call-start = ((), (), s32[]{:S(2)}) async-start(), calls=%async_computation.19 | async-start | bytes 25165824 | tf_op jit(solution)/shard_map/psum | solution.py:193
  875.3 346.9 %all-reduce.7.cloned.1.call-start = ((), (), s32[]{:S(2)}) async-start(), calls=%async_computation.16 | async-start | bytes 8388608 | tf_op jit(solution)/shard_map/psum | solution.py:132
  875.6 239.9 %copy-start.13 = (bf16[512,1024]{1,0:T(8,128)(2,1)S(1)}, bf16[512,1024]{1,0:T(8,128)(2,1)}, u32[]{:S(2)}) copy-start(bf16[512,1024]{1,0:T(8,128)(2,1)} %all-gather.17.cloned.1.call-done) | copy-start | bytes 3145732
  875.6 239.9 %copy-start.15 = (bf16[512,1024]{1,0:T(8,128)(2,1)S(1)}, bf16[512,1024]{1,0:T(8,128)(2,1)}, u32[]{:S(2)}) copy-start(bf16[512,1024]{1,0:T(8,128)(2,1)} %all-gather.15.cloned.1.call-done) | copy-start | bytes 3145732
  875.6 239.9 %copy-start.40 = (f32[3072]{0:T(1024)S(1)}, f32[3072]{0:T(1024)}, u32[]{:S(2)}) copy-start(f32[3072]{0:T(1024)} %copy-done.39) | copy-start | bytes 36868
  875.6 239.9 %copy-start.46 = (f32[1,1024]{1,0:T(1,128)S(1)}, f32[1,1024]{1,0:T(1,128)}, u32[]{:S(2)}) copy-start(f32[1,1024]{1,0:T(1,128)} %copy-done.45) | copy-start | bytes 12292
  887.4 238.0 %copy-start.44 = (f32[3072]{0:T(1024)S(1)}, f32[3072]{0:T(1024)}, u32[]{:S(2)}) copy-start(f32[3072]{0:T(1024)} %copy-done.43) | copy-start | bytes 36868
  887.4 238.0 %copy-start.42 = (f32[3072]{0:T(1024)S(1)}, f32[3072]{0:T(1024)}, u32[]{:S(2)}) copy-start(f32[3072]{0:T(1024)} %copy-done.41) | copy-start | bytes 36868
  887.5 368.5 %reduce-scatter.25.cloned.1.call-start = ((), (), s32[]{:S(2)}) async-start(), calls=%async_computation.27 | async-start | bytes 589824
  1156.4 140.2 %reduce-scatter.11.cloned.1.call-start = ((), (), s32[]{:S(2)}) async-start(), calls=%async_computation.20 | async-start | bytes 3538944 | tf_op jit(solution)/shard_map/reduce_scatter | solution.py:203
  1161.1 187.7 %reduce-scatter.21.cloned.1.call-start = ((), (), s32[]{:S(2)}) async-start(), calls=%async_computation.25 | async-start | bytes 4718592 | tf_op jit(solution)/shard_map/reduce_scatter | solution.py:207
  1171.6 228.3 %reduce-scatter.23.cloned.1.call-start = ((), (), s32[]{:S(2)}) async-start(), calls=%async_computation.26 | async-start | bytes 4718592 | tf_op jit(solution)/shard_map/reduce_scatter | solution.py:211
  1183.9 249.7 %reduce-scatter.19.cloned.1.call-start = ((), (), s32[]{:S(2)}) async-start(), calls=%async_computation.24 | async-start | bytes 1179648 | tf_op jit(solution)/shard_map/reduce_scatter | solution.py:210
  1189.6 277.6 %reduce-scatter.13.cloned.1.call-start = ((), (), s32[]{:S(2)}) async-start(), calls=%async_computation.21 | async-start | bytes 1179648 | tf_op jit(solution)/shard_map/reduce_scatter | solution.py:204
  1194.6 306.4 %reduce-scatter.15.cloned.1.call-start = ((), (), s32[]{:S(2)}) async-start(), calls=%async_computation.22 | async-start | bytes 1179648 | tf_op jit(solution)/shard_map/reduce_scatter | solution.py:205
  1201.2 333.3 %reduce-scatter.17.cloned.1.call-start = ((), (), s32[]{:S(2)}) async-start(), calls=%async_computation.23 | async-start | bytes 1179648 | tf_op jit(solution)/shard_map/reduce_scatter | solution.py:206
  (70 other events, 565.9 us)
Sparse Core Ops, SparseCore 0:
  9.8 46.4 all-gather.10
  58.0 25.2 all-gather.12
  85.1 25.4 all-gather.16
  112.3 52.4 all-gather.8
  167.0 26.3 all-gather.14
  194.9 30.5 all-gather.20
  227.3 51.4 all-gather.22
  302.9 171.9 all-reduce.4
  476.5 29.8 all-gather.18
  531.6 171.4 all-reduce.8
  875.4 239.9 all-reduce.10
  1118.6 103.6 all-reduce.6
  1224.5 31.3 reduce-scatter.24
  1258.1 38.5 reduce-scatter.10
  1299.4 49.3 reduce-scatter.20
  1351.4 48.3 reduce-scatter.22
  1402.5 31.0 reduce-scatter.18
  1436.4 30.8 reduce-scatter.12
  1470.1 30.8 reduce-scatter.14
  1503.7 30.7 reduce-scatter.16
where the time goes:
time: 1550 us; the launch traced here: 1540 us
  waiting for transfers between devices  1000 us (65%)
  matrix products  250 us (16%)
  other arithmetic  142 us (9%)
  blocking collectives  72.7 us (5%)
  local copies, waits for them, and re-layouts  58.5 us (4%)
    psum x1, waiting for transfers between devices, on_device(): grad_normed = lax.psum(partial_rows, 'col')  228 us
    psum x1, waiting for transfers between devices, on_device(): grad_hidden = lax.psum(contract_cols(grad_upper, up_full), 'col')  172 us
    psum x1, waiting for transfers between devices, on_device(): lax.psum(jnp.dot(mixed, proj_full, preferred_element_type=jnp.float32), '...  161 us
    reduce_scatter x1, waiting for transfers between devices, on_device(): lax.psum_scatter(grad_down, 'row', scatter_dimension=1, tiled=True)  51.1 us
    reduce_scatter x1, waiting for transfers between devices, on_device(): lax.psum_scatter(grad_up, 'row', scatter_dimension=0, tiled=True)  50.2 us
    dot_general x8, matrix products, masked_scores(): jnp.einsum('qhd,khd->hqk', query_block, key_heads, preferred_element_type...  49.4 us
    dot_general x7, matrix products, contract_rows(): lax.dot_general(left, right, (((0,), (0,)), ((), ())), preferred_element_...  49.2 us
    all_gather x1, waiting for transfers between devices, on_device(): lax.all_gather(old_memory, 'col', axis=1, tiled=True)  46.2 us
  transfers between devices with their start and end apart: 20, of which 17 were waited for; matrix products, arithmetic and copies ran while one was open for 15% of the time, Pallas kernels for 0%

commit v1 on v0

--- a/solution.py
+++ b/solution.py
@@ -40,6 +40,11 @@
     down_weight,
     cotangent,
 ):
+
+    def scan_row_all(incoming_x):
+        piece_now = jax.lax.all_gather(incoming_x, axis_name="col")
+        return jnp.sum(piece_now, axis=0)
+
     full_tokens, full_memory, full_old, full_grad = (
         lax.all_gather(tokens, "col", axis=1, tiled=True),
         lax.all_gather(memory, "col", axis=1, tiled=True),
@@ -190,7 +195,7 @@
     partial_rows = jnp.concatenate(
         [back_keys[:start_tok], back_keys[start_tok:] + back_queries], axis=0
     )
-    grad_normed = lax.psum(partial_rows, "col")
+    grad_normed = scan_row_all(partial_rows)
     _, first_pull = jax.vjp(normalize, stacked, gain_one)
     grad_stacked, grad_gain_one = first_pull(grad_normed)
     grad_comp_slab = lax.dynamic_slice_in_dim(grad_stacked[:comp_len], column * slab, slab, 1)

time: 1550 us -> 1740 us (1.12)
  waiting for transfers between devices: 1000 us -> 1170 us
  other arithmetic: 142 us -> 167 us
    all_gather x0 -> x1, waiting for transfers between devices: none -> 424 us  [scan_row_all(): piece_now = jax.lax.all_gather(incoming_x, axis_name='col')]
    psum x1 -> x0, waiting for transfers between devices: 228 us -> none  [on_device(): grad_normed = lax.psum(partial_rows, 'col')]
    reduce_sum x0 -> x1, other arithmetic: none -> 24.8 us  [scan_row_all(): return jnp.sum(piece_now, axis=0)]
  transfers between devices with their start and end apart: 20 -> 20, of which waited for: 17 -> 16; matrix products, arithmetic and copies ran while one was open for 15% -> 15% of each run, Pallas kernels for 0% -> 0%
where the time goes in v1:
time: 1740 us
  waiting for transfers between devices  1170 us (67%)
  matrix products  250 us (14%)
  other arithmetic  167 us (10%)
  blocking collectives  72.7 us (4%)
  local copies, waits for them, and re-layouts  59.3 us (3%)
    all_gather x1, waiting for transfers between devices, scan_row_all(): piece_now = jax.lax.all_gather(incoming_x, axis_name='col')  424 us
    psum x1, waiting for transfers between devices, on_device(): grad_hidden = lax.psum(contract_cols(grad_upper, up_full), 'col')  172 us
    psum x1, waiting for transfers between devices, on_device(): lax.psum(jnp.dot(mixed, proj_full, preferred_element_type=jnp.float32), '...  161 us
    reduce_scatter x1, waiting for transfers between devices, on_device(): lax.psum_scatter(grad_down, 'row', scatter_dimension=1, tiled=True)  51.1 us
    reduce_scatter x1, waiting for transfers between devices, on_device(): lax.psum_scatter(grad_up, 'row', scatter_dimension=0, tiled=True)  50 us
    dot_general x7, matrix products, contract_rows(): lax.dot_general(left, right, (((0,), (0,)), ((), ())), preferred_element_...  49.5 us
    dot_general x8, matrix products, masked_scores(): jnp.einsum('qhd,khd->hqk', query_block, key_heads, preferred_element_type...  49.3 us
    all_gather x1, waiting for transfers between devices, on_device(): lax.all_gather(old_memory, 'col', axis=1, tiled=True)  46.2 us
  transfers between devices with their start and end apart: 20, of which 16 were waited for; matrix products, arithmetic and copies ran while one was open for 15% of the time, Pallas kernels for 0%

profile of v1, /device:TPU:0, one launch (start us, length us, event | category | flops | bytes accessed | tf_op | source)
XLA Modules:
  0.0 1738.3 jit_solution(6438237873518996908)
XLA Ops:
  10.1 46.2 %all-gather.13.cloned.1.call-done = bf16[1536,1024]{1,0:T(8,128)(2,1)} async-done(((bf16[1536,256]{1,0:T(8,128)(2,1)}), bf16[1536,1024]{1,0:T(8,128)(2,1)}) %all-gather.13.cloned.1.call-update) | async-done | bytes 3145744 | tf_op jit(solution)/shard_map/all_gather | solution.py:51
  60.6 22.7 %all-gather.15.cloned.1.call-done = bf16[3072,256]{1,0:T(8,128)(2,1)} async-done(((bf16[384,256]{1,0:T(8,128)(2,1)}), bf16[3072,256]{1,0:T(8,128)(2,1)}) %all-gather.15.cloned.1.call-update) | async-done | bytes 1572880 | tf_op jit(solution)/shard_map/all_gather | solution.py:55
  88.0 9.9 all_gather.50
  98.6 15.8 all_gather.51
  114.4 15.8 all_gather.52
  130.2 15.8 all_gather.53
  146.1 15.2 all_gather.54
  164.8 28.6 %all-gather.17.cloned.1.call-done = bf16[512,1024]{1,0:T(8,128)(2,1)} async-done(((bf16[512,256]{1,0:T(8,128)(2,1)}), bf16[512,1024]{1,0:T(8,128)(2,1)}) %all-gather.17.cloned.1.call-update) | async-done | bytes 1048592 | tf_op jit(solution)/shard_map/all_gather | solution.py:80
  232.0 61.1 %while.30 = (s32[]{:T(128)}, bf16[4,512,2,128]{3,1,2,0:T(8,128)(2,1)}, f32[4,2,512,1]{2,1,3,0:T(2,128)S(1)}, f32[4,2,512,1]{2,1,3,0:T(2,128)S(1)}, s32[4,512]{1,...) while((s32[]{:T(128)}, ...), condition=%wide.region_5.6_spmd.clone, body=%wide.region_2.5_spmd.clone.sunk | while | flops 1653081088 | bytes 56447168 | solution.py:129
  303.6 10.7 fusion.78
  314.3 160.6 %all-reduce.4.cloned.1.call-done = f32[2048,1024]{1,0:T(8,128)} async-done(((f32[2048,1024]{1,0:T(8,128)}), f32[2048,1024]{1,0:T(8,128)}) %all-reduce.4.cloned.1.call-update) | async-done | bytes 8388624 | tf_op jit(solution)/shard_map/psum | solution.py:131
  486.2 20.2 %all-gather.21.cloned.1.call-done = bf16[1024,1024]{1,0:T(8,128)(2,1)} async-done(((bf16[128,1024]{1,0:T(8,128)(2,1)}), bf16[1024,1024]{1,0:T(8,128)(2,1)}) %all-gather.21.cloned.1.call-update) | async-done | bytes 2097168 | tf_op jit(solution)/shard_map/all_gather | solution.py:59
  506.4 15.9 fusion.50
  531.4 171.5 %all-reduce.8.cloned.1.call-done = f32[2048,1024]{1,0:T(8,128)} async-done(((f32[2048,1024]{1,0:T(8,128)}), f32[2048,1024]{1,0:T(8,128)}) %all-reduce.8.cloned.1.call-update) | async-done | bytes 8388624 | tf_op jit(solution)/shard_map/psum | solution.py:144
  726.1 122.1 %while.31 = (s32[]{:T(128)}, f32[3072,2,128]{0,2,1:T(8,128)S(1)}, f32[3072,2,128]{0,2,1:T(8,128)}, bf16[4,512,2,128]{3,1,2,0:T(8,128)(2,1)}, bf16[4,512,2,128]{3...) while((s32[]{:T(128)}, f32[3072,2,128]{0,2,1:T(8,128)S(1)}, ...), condition=%wide.region_15.16_spmd.clone, body=%wide.region_13.15_spmd.clone.sunk | while | flops 4066772992 | bytes 161038704 | solution.py:182
  863.1 11.8 pad_maximum_fusion
  876.5 12.2 convolution_convert_fusion.2
  888.7 423.9 %all-gather.27.cloned.1.call-done = f32[12288,1024]{1,0:T(8,128)} async-done(((f32[3072,1024]{1,0:T(8,128)}), f32[12288,1024]{1,0:T(8,128)}) %all-gather.27.cloned.1.call-update) | async-done | bytes 50331664 | tf_op jit(solution)/shard_map/all_gather | solution.py:45
  1312.7 24.8 %reduce_sum.127 = f32[3072,1024]{1,0:T(8,128)} reduce(f32[4,3072,1024]{2,1,0:T(8,128)} %bitcast.156, f32[]{:T(128)} %constant.78.clone.1), dimensions={0}, to_apply=%region_16.17 | reduce | flops 9437184 | bytes 62914564 | tf_op jit(solution)/shard_map/reduce_sum | solution.py:46
  1337.6 10.2 fusion.43
  1348.7 11.9 fusion.41
  1361.7 11.4 broadcast_add_fusion
  1383.4 10.0 fusion.83
  1393.5 13.0 fusion.74
  1438.8 14.3 reduce-scatter.25.cloned.1.call-done
  1454.6 39.1 %reduce-scatter.11.cloned.1.call-done = f32[384,256]{0,1:T(8,128)} async-done(((f32[3072,256]{0,1:T(8,128)}), f32[384,256]{0,1:T(8,128)}) %reduce-scatter.11.cloned.1.call-update) | async-done | bytes 393232 | tf_op jit(solution)/shard_map/reduce_scatter | solution.py:208
  1495.6 50.0 %reduce-scatter.21.cloned.1.call-done = f32[128,1024]{1,0:T(8,128)} async-done(((f32[1024,1024]{1,0:T(8,128)}), f32[128,1024]{1,0:T(8,128)}) %reduce-scatter.21.cloned.1.call-update) | async-done | bytes 524304 | tf_op jit(solution)/shard_map/reduce_scatter | solution.py:212
  1545.6 51.1 %reduce-scatter.23.cloned.1.call-done = f32[1024,128]{1,0:T(8,128)} async-done(((f32[1024,1024]{1,0:T(8,128)}), f32[1024,128]{1,0:T(8,128)}) %reduce-scatter.23.cloned.1.call-update) | async-done | bytes 524304 | tf_op jit(solution)/shard_map/reduce_scatter | solution.py:216
  1596.7 33.8 %reduce-scatter.19.cloned.1.call-done = f32[256,128]{1,0:T(8,128)} async-done(((f32[256,1024]{1,0:T(8,128)}), f32[256,128]{1,0:T(8,128)}) %reduce-scatter.19.cloned.1.call-update) | async-done | bytes 131088 | tf_op jit(solution)/shard_map/reduce_scatter | solution.py:215
  1630.5 33.6 %reduce-scatter.13.cloned.1.call-done = f32[128,256]{1,0:T(8,128)} async-done(((f32[1024,256]{1,0:T(8,128)}), f32[128,256]{1,0:T(8,128)}) %reduce-scatter.13.cloned.1.call-update) | async-done | bytes 131088 | tf_op jit(solution)/shard_map/reduce_scatter | solution.py:209
  1664.1 33.7 %reduce-scatter.15.cloned.1.call-done = f32[128,256]{1,0:T(8,128)} async-done(((f32[1024,256]{1,0:T(8,128)}), f32[128,256]{1,0:T(8,128)}) %reduce-scatter.15.cloned.1.call-update) | async-done | bytes 131088 | tf_op jit(solution)/shard_map/reduce_scatter | solution.py:210
  1697.7 33.5 %reduce-scatter.17.cloned.1.call-done = f32[128,256]{1,0:T(8,128)} async-done(((f32[1024,256]{1,0:T(8,128)}), f32[128,256]{1,0:T(8,128)}) %reduce-scatter.17.cloned.1.call-update) | async-done | bytes 131088 | tf_op jit(solution)/shard_map/reduce_scatter | solution.py:211
  (350 shorter events, 354.3 us)
Async XLA Ops:
  7.2 80.6 %copy-start.52 = (s32[1,4096]{1,0:T(1,128)S(1)}, s32[1,4096]{1,0:T(1,128)}, u32[]{:S(2)}) copy-start(s32[1,4096]{1,0:T(1,128)} %param.20) | copy-start | bytes 49156
  7.2 80.8 %copy-start.54 = (bf16[2,128]{1,0:T(2,128)(2,1)S(1)}, bf16[2,128]{1,0:T(2,128)(2,1)}, u32[]{:S(2)}) copy-start(bf16[2,128]{1,0:T(2,128)(2,1)} %param.21) | copy-start | bytes 1540
  7.2 91.4 %copy-start.47 = (bf16[128,256]{1,0:T(8,128)(2,1)S(1)}, bf16[128,256]{1,0:T(8,128)(2,1)}, u32[]{:S(2)}) copy-start(bf16[128,256]{1,0:T(8,128)(2,1)} %param.23) | copy-start | bytes 196612
  7.2 107.2 %copy-start.48 = (bf16[128,256]{1,0:T(8,128)(2,1)S(1)}, bf16[128,256]{1,0:T(8,128)(2,1)}, u32[]{:S(2)}) copy-start(bf16[128,256]{1,0:T(8,128)(2,1)} %param.24) | copy-start | bytes 196612
  7.2 49.1 %all-gather.13.cloned.1.call-start = ((), (), s32[]{:S(2)}) async-start(), calls=%async_computation.9 | async-start | bytes 3932160 | tf_op jit(solution)/shard_map/all_gather | solution.py:51
  8.0 122.3 %copy-start.49 = (bf16[128,256]{1,0:T(8,128)(2,1)S(1)}, bf16[128,256]{1,0:T(8,128)(2,1)}, u32[]{:S(2)}) copy-start(bf16[128,256]{1,0:T(8,128)(2,1)} %param.25) | copy-start | bytes 196612
  8.0 75.3 %all-gather.15.cloned.1.call-start = ((), (), s32[]{:S(2)}) async-start(), calls=%async_computation.10 | async-start | bytes 1769472 | tf_op jit(solution)/shard_map/all_gather | solution.py:55
  8.7 152.6 %all-gather.19.cloned.1.call-start = ((), (), s32[]{:S(2)}) async-start(), calls=%async_computation.12 | async-start | bytes 1310720 | tf_op jit(solution)/shard_map/all_gather | solution.py:50
  9.4 136.6 %copy-start.50 = (bf16[256,128]{1,0:T(8,128)(2,1)S(1)}, bf16[256,128]{1,0:T(8,128)(2,1)}, u32[]{:S(2)}) copy-start(bf16[256,128]{1,0:T(8,128)(2,1)} %param.26) | copy-start | bytes 196612
  9.5 155.3 %all-gather.11.cloned.1.call-start = ((), (), s32[]{:S(2)}) async-start(), calls=%async_computation.8 | async-start | bytes 5242880 | tf_op jit(solution)/shard_map/all_gather | solution.py:49
  10.0 183.4 %all-gather.17.cloned.1.call-start = ((), (), s32[]{:S(2)}) async-start(), calls=%async_computation.11 | async-start | bytes 1310720 | tf_op jit(solution)/shard_map/all_gather | solution.py:80
  60.5 100.8 %copy-start.19 = (bf16[512,3072]{1,0:T(8,128)(2,1)}, bf16[512,3072]{1,0:T(8,128)(2,1)S(1)}, u32[]{:S(2)}) copy-start(bf16[512,3072]{1,0:T(8,128)(2,1)S(1)} %reshape.251) | copy-start | bytes 9437188
  86.4 217.2 %all-gather.23.cloned.1.call-start = ((), (), s32[]{:S(2)}) async-start(), calls=%async_computation.15 | async-start | bytes 2359296 | tf_op jit(solution)/shard_map/all_gather | solution.py:63
  86.9 216.7 %all-gather.25.cloned.1.call-start = ((), (), s32[]{:S(2)}) async-start(), calls=%async_computation.17 | async-start | bytes 5242880 | tf_op jit(solution)/shard_map/all_gather | solution.py:52
  87.7 387.2 %all-reduce.4.cloned.1.call-start = ((), (), s32[]{:S(2)}) async-start(), calls=%async_computation.13 | async-start | bytes 16777216 | tf_op jit(solution)/shard_map/psum | solution.py:131
  98.5 111.4 %copy-start.45 = (f32[1,1024]{1,0:T(1,128)}, f32[1,1024]{1,0:T(1,128)S(1)}, u32[]{:S(2)}) copy-start(f32[1,1024]{1,0:T(1,128)S(1)} %get-tuple-element.379) | copy-start | bytes 12292
  161.3 42.7 %copy-start.12 = (bf16[512,1024]{1,0:T(8,128)(2,1)S(1)}, bf16[512,1024]{1,0:T(8,128)(2,1)}, u32[]{:S(2)}) copy-start(bf16[512,1024]{1,0:T(8,128)(2,1)} %all-gather.19.cloned.1.call-done) | copy-start | bytes 3145732
  302.8 203.6 %all-gather.21.cloned.1.call-start = ((), (), s32[]{:S(2)}) async-start(), calls=%async_computation.14 | async-start | bytes 2359296 | tf_op jit(solution)/shard_map/all_gather | solution.py:59
  303.5 399.3 %all-reduce.8.cloned.1.call-start = ((), (), s32[]{:S(2)}) async-start(), calls=%async_computation.18 | async-start | bytes 16777216 | tf_op jit(solution)/shard_map/psum | solution.py:144
  531.3 781.4 %all-gather.27.cloned.1.call-start = ((), (), s32[]{:S(2)}) async-start(), calls=%async_computation.26 | async-start | bytes 62914560 | tf_op jit(solution)/shard_map/all_gather | solution.py:45
  874.9 554.0 %all-reduce.6.cloned.1.call-start = ((), (), s32[]{:S(2)}) async-start(), calls=%async_computation.16 | async-start | bytes 8388608 | tf_op jit(solution)/shard_map/psum | solution.py:137
  888.7 564.5 %reduce-scatter.25.cloned.1.call-start = ((), (), s32[]{:S(2)}) async-start(), calls=%async_computation.27 | async-start | bytes 589824
  1312.7 24.9 %copy-start.15 = (bf16[512,1024]{1,0:T(8,128)(2,1)S(1)}, bf16[512,1024]{1,0:T(8,128)(2,1)}, u32[]{:S(2)}) copy-start(bf16[512,1024]{1,0:T(8,128)(2,1)} %all-gather.17.cloned.1.call-done) | copy-start | bytes 3145732
  1312.7 24.9 %copy-start.40 = (f32[3072]{0:T(1024)S(1)}, f32[3072]{0:T(1024)}, u32[]{:S(2)}) copy-start(f32[3072]{0:T(1024)} %copy-done.39) | copy-start | bytes 36868
  1312.7 24.9 %copy-start.46 = (f32[1,1024]{1,0:T(1,128)S(1)}, f32[1,1024]{1,0:T(1,128)}, u32[]{:S(2)}) copy-start(f32[1,1024]{1,0:T(1,128)} %copy-done.45) | copy-start | bytes 12292
  1378.3 115.4 %reduce-scatter.11.cloned.1.call-start = ((), (), s32[]{:S(2)}) async-start(), calls=%async_computation.19 | async-start | bytes 3538944 | tf_op jit(solution)/shard_map/reduce_scatter | solution.py:208
  1383.3 162.3 %reduce-scatter.21.cloned.1.call-start = ((), (), s32[]{:S(2)}) async-start(), calls=%async_computation.24 | async-start | bytes 4718592 | tf_op jit(solution)/shard_map/reduce_scatter | solution.py:212
  1393.4 203.3 %reduce-scatter.23.cloned.1.call-start = ((), (), s32[]{:S(2)}) async-start(), calls=%async_computation.25 | async-start | bytes 4718592 | tf_op jit(solution)/shard_map/reduce_scatter | solution.py:216
  1406.4 224.1 %reduce-scatter.19.cloned.1.call-start = ((), (), s32[]{:S(2)}) async-start(), calls=%async_computation.23 | async-start | bytes 1179648 | tf_op jit(solution)/shard_map/reduce_scatter | solution.py:215
  1412.3 251.7 %reduce-scatter.13.cloned.1.call-start = ((), (), s32[]{:S(2)}) async-start(), calls=%async_computation.20 | async-start | bytes 1179648 | tf_op jit(solution)/shard_map/reduce_scatter | solution.py:209
  1417.5 280.3 %reduce-scatter.15.cloned.1.call-start = ((), (), s32[]{:S(2)}) async-start(), calls=%async_computation.21 | async-start | bytes 1179648 | tf_op jit(solution)/shard_map/reduce_scatter | solution.py:210
  1423.3 308.0 %reduce-scatter.17.cloned.1.call-start = ((), (), s32[]{:S(2)}) async-start(), calls=%async_computation.22 | async-start | bytes 1179648 | tf_op jit(solution)/shard_map/reduce_scatter | solution.py:211
  (71 other events, 409.2 us)
Sparse Core Ops, SparseCore 0:
  9.8 46.4 all-gather.12
  58.0 25.2 all-gather.14
  85.1 25.4 all-gather.18
  112.3 52.4 all-gather.10
  167.0 26.3 all-gather.16
  194.9 30.5 all-gather.22
  227.3 51.4 all-gather.24
  302.9 171.9 all-reduce.3
  476.5 29.8 all-gather.20
  531.4 171.4 all-reduce.7
  875.1 437.5 all-gather.26
  1315.8 103.5 all-reduce.5
  1421.7 31.3 reduce-scatter.24
  1455.3 38.3 reduce-scatter.10
  1496.4 49.1 reduce-scatter.20
  1548.3 48.3 reduce-scatter.22
  1599.4 31.0 reduce-scatter.18
  1633.2 30.8 reduce-scatter.12
  1666.9 30.7 reduce-scatter.14
  1700.4 30.7 reduce-scatter.16
